TPU v7x, 32 devices: a whole 2x2x4 slice. The times are simulated.
32 devices in a mesh: row: 8 (over z, x), col: 4 (over y, core).
Axes of the slice: x: 2, y: 2, z: 4, core: 2. Of those that a mesh axis runs over, the one named last changes fastest.
Arguments:
- features: bfloat16 [32768, 256], P(('col', 'row')), may hold values from -6 to 6
- adjacency: bfloat16 [256, 4, 12, 128, 128], P('row', 'col'), may hold values from 0 to 0.023925781
- block_cols: int32 [256, 4, 12], P('row', 'col'), may hold values from 0 to 63, as said below
- block_live: int32 [256, 4], P('row', 'col'), may hold values from 1 to 12, as said below
- weight: bfloat16 [256, 256], replicated, may hold values from -0.375 to 0.375
- bias: float32 [256], replicated, may hold values from -3 to 3
- upstream: bfloat16 [32768, 256], P(('row', 'col')), may hold values from -6 to 6
Outputs:
- activations: bfloat16 [32768, 256], P(('row', 'col'))
- feature_grad: bfloat16 [32768, 256], P(('col', 'row'))
- weight_grad: float32 [256, 256], replicated
- bias_grad: float32 [256], replicated
Inputs may be any that keep to these rules, and one draw needn't show every extreme that they name: `block_cols`: the live slots of one block row in one column tile name distinct column blocks of that tile. Slots k with k < block_live[i, c] are live; the other slots of block_cols and adjacency are ignored. Some entry equals 12.
All inputs are finite; a program needn't handle non-finite values.
Results may differ from a plain program's by a relative error of at most 0.014.
Values may be sent and summed in bfloat16 or wider, within the bound.
No kernel may reach another device: no remote copies, remote signals or barrier semaphores. Data moves between devices by JAX's collectives and lax.ppermute only.
A program may use at most 256 MiB of HBM per device.

v0:
```python
import jax
import jax.numpy as jnp
from jax import lax
from jax.sharding import PartitionSpec as P


def local(features, adjacency, block_cols, block_live, weight, bias, upstream):
    block_rows = adjacency.shape[0]
    block_slots = adjacency.shape[2]
    block_size = adjacency.shape[3]
    feature_width = features.shape[1]
    tile_blocks = adjacency.reshape(block_rows, block_slots, block_size, block_size)
    column_ids = block_cols.reshape(block_rows, block_slots)
    live_count = block_live.reshape(block_rows)
    live_mask = lax.broadcasted_iota(jnp.int32, (block_rows, block_slots), 1) < live_count[:, None]
    feature_panel = lax.all_gather(features, "row", axis=0, tiled=True)
    panel_blocks = feature_panel.shape[0] // block_size
    picked = feature_panel.reshape(panel_blocks, block_size, feature_width)[column_ids]
    picked = jnp.where(live_mask[:, :, None, None], picked, jnp.zeros((), jnp.bfloat16))
    partial_value = jnp.einsum(
        "ikab,ikbf->iaf", tile_blocks, picked, preferred_element_type=jnp.float32
    )
    partial_value = partial_value.reshape(block_rows * block_size, feature_width)
    aggregated = lax.psum_scatter(partial_value, "col", scatter_dimension=0, tiled=True).astype(
        jnp.bfloat16
    )
    preact = jnp.dot(aggregated, weight, preferred_element_type=jnp.float32) + bias
    sigmoid_pre = jax.nn.sigmoid(preact)
    outputs_here = (preact * sigmoid_pre).astype(jnp.bfloat16)
    derivative = sigmoid_pre * (1.0 + preact * (1.0 - sigmoid_pre))
    grad_pre = (upstream.astype(jnp.float32) * derivative).astype(jnp.bfloat16)
    weight_part = jnp.einsum("nf,ng->fg", aggregated, grad_pre, preferred_element_type=jnp.float32)
    bias_part = jnp.sum(grad_pre.astype(jnp.float32), axis=0)
    grad_agg = jnp.einsum("ng,fg->nf", grad_pre, weight, preferred_element_type=jnp.float32).astype(
        jnp.bfloat16
    )
    weight_grad, bias_grad = lax.psum((weight_part, bias_part), ("row", "col"))
    tile_grad = lax.all_gather(grad_agg, "col", axis=0, tiled=True)
    contrib = jnp.einsum(
        "ikab,iaf->ikbf",
        tile_blocks,
        tile_grad.reshape(block_rows, block_size, feature_width),
        preferred_element_type=jnp.float32,
    )
    contrib = contrib.reshape(block_rows * block_slots, block_size, feature_width)
    target_blocks = jnp.where(live_mask, column_ids, panel_blocks).reshape(-1)
    panel_sum = jnp.zeros((panel_blocks, block_size, feature_width), jnp.float32)
    panel_sum = panel_sum.at[target_blocks].add(contrib, mode="drop")
    panel_sum = panel_sum.reshape(panel_blocks * block_size, feature_width)
    feature_grad = lax.psum_scatter(
        panel_sum.astype(jnp.bfloat16), "row", scatter_dimension=0, tiled=True
    )
    return (outputs_here, feature_grad, weight_grad, bias_grad)


def solution(mesh):
    placed = (
        P(("col", "row"), None),
        P("row", "col", None, None, None),
        P("row", "col", None),
        P("row", "col"),
        P(),
        P(),
        P(("row", "col"), None),
    )
    return jax.shard_map(
        local,
        mesh=mesh,
        in_specs=placed,
        out_specs=(P(("row", "col"), None), P(("col", "row"), None), P(), P()),
        check_vma=False,
    )
```

profile of v0, /device:TPU:0, one launch (start us, length us, event | category | flops | bytes accessed | tf_op | source)
XLA Modules:
  0.0 477.4 jit_solution(3709703805803400464)
XLA Ops:
  7.2 0.7 all-gather.3.cloned.1.call-update
  8.0 0.7 compare_select_fusion
  8.7 0.1 copy.12
  8.8 0.1 reshape.129
  8.9 0.7 iota_compare_fusion
  9.6 76.1 %all-gather.3.cloned.1.call-done = bf16[8192,256]{1,0:T(8,128)(2,1)} async-done(((bf16[1024,256]{1,0:T(8,128)(2,1)}), bf16[8192,256]{1,0:T(8,128)(2,1)}) %all-gather.3.cloned.1.call-update) | async-done | bytes 4194320 | tf_op jit(solution)/shard_map/all_gather | solution.py:16
  85.7 15.1 %gather_fusion = bf16[384,128,256]{2,1,0:T(8,128)(2,1)} fusion(bf16[64,128,256]{2,1,0:T(8,128)(2,1)} %bitcast.35, s32[1024]{0:T(1024)S(1)} %pad_clamp_fusion), kind=kCustom, calls=%fused_computation | custom fusion | bytes 50333184 | tf_op jit(solution)/shard_map/gather | solution.py:18
  100.8 16.1 %fusion = f32[32,256,128,1]{1,2,3,0:T(8,128)} fusion(bf16[32,12,128,256]{3,2,1,0:T(8,128)(2,1)} %bitcast.36, pred[32,12]{1,0:T(8,128)(4,1)S(1)} %iota_compare_fusion, bf16[32,1,12,128,128]{4,3,2,1,0:T(8,128)(2,1)} %param.8), kind=kOutput, calls=%fused_computation.2 | convolution fusion | flops 3233808384 | bytes 41943424 | tf_op jit(solution)/shard_map/ikab,ikbf->iaf/dot_general | solution.py:20
  116.9 43.2 %reduce-scatter.3.cloned.1.call-done = f32[1024,256]{1,0:T(8,128)} async-done(((f32[4096,256]{1,0:T(8,128)}), f32[1024,256]{1,0:T(8,128)}) %reduce-scatter.3.cloned.1.call-update) | async-done | bytes 1048592 | tf_op jit(solution)/shard_map/reduce_scatter | solution.py:24
  160.2 2.7 convert_reduce_fusion
  162.9 1.1 convolution_convert_fusion
  164.1 0.1 lt.53
  164.2 0.1 copy.13
  164.3 0.1 reshape.124
  164.4 2.3 fusion.7
  166.8 20.0 %all-gather.5.cloned.1.call-done = bf16[4096,256]{1,0:T(8,128)(2,1)} async-done(((bf16[1024,256]{1,0:T(8,128)(2,1)}), bf16[4096,256]{1,0:T(8,128)(2,1)}) %all-gather.5.cloned.1.call-update) | async-done | bytes 2097168 | tf_op jit(solution)/shard_map/all_gather | solution.py:38
  186.7 22.5 %fusion.3 = f32[32,256,12,128]{3,1,2,0:T(8,128)} fusion(bf16[32,128,256,1]{2,1,3,0:T(8,128)(2,1)} %bitcast.39, bf16[32,1,12,128,128]{4,3,2,1,0:T(8,128)(2,1)} %param.8), kind=kOutput, calls=%fused_computation.5 | convolution fusion | flops 3221225472 | bytes 65011712 | tf_op jit(solution)/shard_map/ikab,iaf->ikbf/dot_general | solution.py:39
  209.3 48.9 %copy.15 = f32[384,128,256]{2,1,0:T(8,128)} copy(f32[384,128,256]{1,2,0:T(8,128)} %bitcast.34) | data formatting | bytes 100663296 | tf_op jit(solution)/shard_map/reshape | solution.py:45
  258.2 4.2 broadcast_in_dim.23
  262.4 109.8 %scatter_fusion = f32[64,128,256]{2,1,0:T(8,128)} fusion(f32[64,128,256]{2,1,0:T(8,128)} %broadcast_in_dim.23, s32[384]{0:T(512)S(1)} %fusion.10, f32[384,128,256]{2,1,0:T(8,128)} %copy.15), kind=kCustom, calls=%fused_computation.1 | custom fusion | flops 12582912 | bytes 150996480 | tf_op jit(solution)/shard_map/scatter-add | solution.py:48
  372.2 5.9 %convert_element_type.29 = bf16[64,128,256]{2,1,0:T(8,128)(2,1)} convert(f32[64,128,256]{2,1,0:T(8,128)} %scatter_fusion) | non-fusion elementwise | flops 2097152 | bytes 12582912 | tf_op jit(solution)/shard_map/convert_element_type | solution.py:51
  378.1 43.6 %psum.15 = f32[256]{0:T(256)} all-reduce(f32[256]{0:T(256)S(1)} %get-tuple-element.4), channel_id=1, replica_groups=mesh['row'=8,'col'=4] {'row','col'}, use_global_device_ids=true, to_apply=%region_5.6 | all-reduce | flops 256 | bytes 2048 | tf_op jit(solution)/shard_map/psum | solution.py:37
  421.8 47.4 %reduce-scatter.5.cloned.1.call-done = bf16[1024,256]{1,0:T(8,128)(2,1)} async-done(((bf16[8192,256]{1,0:T(8,128)(2,1)}), bf16[1024,256]{1,0:T(8,128)(2,1)}) %reduce-scatter.5.cloned.1.call-update) | async-done | bytes 524304 | tf_op jit(solution)/shard_map/reduce_scatter | solution.py:50
  469.2 1.7 copy.22
  (22 shorter events, 0.3 us)
Async XLA Ops:
  7.2 153.0 %copy-start = (bf16[256,256]{1,0:T(8,128)(2,1)S(1)}, bf16[256,256]{1,0:T(8,128)(2,1)}, u32[]{:S(2)}) copy-start(bf16[256,256]{1,0:T(8,128)(2,1)} %param.11) | copy-start | bytes 393220
  7.2 78.5 %all-gather.3.cloned.1.call-start = ((), (), s32[]{:S(2)}) async-start(), calls=%async_computation.2 | async-start | bytes 4718592 | tf_op jit(solution)/shard_map/all_gather | solution.py:16
  7.9 152.3 %reduce-scatter.3.cloned.1.call-start = ((), (), s32[]{:S(2)}) async-start(), calls=%async_computation.3 | async-start | bytes 5242880 | tf_op jit(solution)/shard_map/reduce_scatter | solution.py:24
  100.8 59.4 %copy-start.3 = (bf16[1024,256]{1,0:T(8,128)(2,1)S(1)}, bf16[1024,256]{1,0:T(8,128)(2,1)}, u32[]{:S(2)}) copy-start(bf16[1024,256]{1,0:T(8,128)(2,1)} %param.13) | copy-start | bytes 1572868
  100.8 59.4 %copy-start.4 = (f32[256]{0:T(256)S(1)}, f32[256]{0:T(256)}, u32[]{:S(2)}) copy-start(f32[256]{0:T(256)} %param.12) | copy-start | bytes 3076
  116.9 47.3 %copy-start.2 = (s32[32,1,12]{0,1,2:T(1,128)S(1)}, s32[32,1,12]{0,1,2:T(1,128)}, u32[]{:S(2)}) copy-start(s32[32,1,12]{0,1,2:T(1,128)} %param.9) | copy-start | bytes 4612
  116.9 69.9 %all-gather.5.cloned.1.call-start = ((), (), s32[]{:S(2)}) async-start(), calls=%async_computation.4 | async-start | bytes 2621440 | tf_op jit(solution)/shard_map/all_gather | solution.py:38
  164.0 257.8 %all-reduce.2.cloned.1.call-start = ((), (), s32[]{:S(2)}) async-start(), calls=%async_computation.6 | async-start | bytes 524288 | tf_op jit(solution)/shard_map/psum | solution.py:37
  166.7 302.4 %reduce-scatter.5.cloned.1.call-start = ((), (), s32[]{:S(2)}) async-start(), calls=%async_computation.5 | async-start | bytes 4718592 | tf_op jit(solution)/shard_map/reduce_scatter | solution.py:50
  262.4 208.4 %copy-start.1 = (bf16[256,256]{1,0:T(8,128)(2,1)S(1)}, bf16[256,256]{1,0:T(8,128)(2,1)}, u32[]{:S(2)}) copy-start(bf16[256,256]{1,0:T(8,128)(2,1)} %param.11) | copy-start | bytes 393220
Sparse Core Ops, SparseCore 0:
  10.1 75.4 all-gather.2
  117.0 43.1 reduce-scatter.2
  164.2 22.5 all-gather.4
  192.7 126.5 all-reduce.1
  378.3 90.8 reduce-scatter.4
where the time goes:
time: 479 us; the launch traced here: 477 us
  waiting for transfers between devices  187 us (39%)
  other arithmetic  117 us (24%)
  local copies, waits for them, and re-layouts  70.4 us (15%)
  matrix products  44.7 us (9%)
  blocking collectives  43.6 us (9%)
  between operations  13.8 us (3%)
    scatter-add x1, other arithmetic, local(): panel_sum = panel_sum.at[target_blocks].add(contrib, mode='drop')  110 us
    all_gather x1, waiting for transfers between devices, local(): feature_panel = lax.all_gather(features, 'row', axis=0, tiled=True)  76.1 us
    reshape x1, local copies, waits for them, and re-layouts, local(): contrib.reshape(block_rows * block_slots, block_size, feature_width)  48.9 us
    reduce_scatter x1, waiting for transfers between devices, local(): lax.psum_scatter(panel_sum.astype(jnp.bfloat16), 'row', scatter_dimension...  47.4 us
    psum x1, blocking collectives, local(): weight_grad, bias_grad = lax.psum((weight_part, bias_part), ('row', 'col'))  43.6 us
    reduce_scatter x1, waiting for transfers between devices, local(): lax.psum_scatter(partial_value, 'col', scatter_dimension=0, tiled=True)  43.2 us
    dot_general x1, matrix products, local(): jnp.einsum('ikab,iaf->ikbf', tile_blocks, tile_grad.reshape(block_rows, b...  22.5 us
    all_gather x1, waiting for transfers between devices, local(): tile_grad = lax.all_gather(grad_agg, 'col', axis=0, tiled=True)  20 us
  transfers between devices with their start and end apart: 5, of which 4 were waited for; matrix products, arithmetic and copies ran while one was open for 41% of the time, Pallas kernels for 0%

commit v1 on v0

--- a/solution.py
+++ b/solution.py
@@ -13,7 +13,12 @@
     column_ids = block_cols.reshape(block_rows, block_slots)
     live_count = block_live.reshape(block_rows)
     live_mask = lax.broadcasted_iota(jnp.int32, (block_rows, block_slots), 1) < live_count[:, None]
-    feature_panel = lax.all_gather(features, "row", axis=0, tiled=True)
+    ring = [features]
+    for hop in range(7):
+        ring.append(lax.ppermute(ring[-1], "row", [(dev, (dev + 1) % 8) for dev in range(8)]))
+    feature_panel = jnp.roll(
+        jnp.concatenate(ring[::-1], axis=0), (lax.axis_index("row") + 1) * ring[0].shape[0], axis=0
+    )
     panel_blocks = feature_panel.shape[0] // block_size
     picked = feature_panel.reshape(panel_blocks, block_size, feature_width)[column_ids]
     picked = jnp.where(live_mask[:, :, None, None], picked, jnp.zeros((), jnp.bfloat16))

time: 479 us -> 507 us (1.058)
  waiting for transfers between devices: 187 us -> 206 us
  local copies, waits for them, and re-layouts: 70.4 us -> 78.5 us
    ppermute x0 -> x7, waiting for transfers between devices: none -> 96.2 us  [local(): lax.ppermute(ring[-1], 'row', [(dev, (dev + 1) % 8) for dev in range(8)])]
    all_gather x1 -> x0, waiting for transfers between devices: 76.1 us -> none  [local(): feature_panel = lax.all_gather(features, 'row', axis=0, tiled=True)]
    unnamed x12 -> x31, local copies, waits for them, and re-layouts: 1.78 us -> 7.54 us
  transfers between devices with their start and end apart: 5 -> 11, of which waited for: 4 -> 10; matrix products, arithmetic and copies ran while one was open for 41% -> 38% of each run, Pallas kernels for 0% -> 0%
where the time goes in v1:
time: 507 us; the launch traced here: 506 us
  waiting for transfers between devices  206 us (41%)
  other arithmetic  116 us (23%)
  local copies, waits for them, and re-layouts  78.5 us (15%)
  blocking collectives  44.5 us (9%)
  matrix products  43.6 us (9%)
  between operations  14 us (3%)
    scatter-add x1, other arithmetic, local(): panel_sum = panel_sum.at[target_blocks].add(contrib, mode='drop')  109 us
    ppermute x7, waiting for transfers between devices, local(): lax.ppermute(ring[-1], 'row', [(dev, (dev + 1) % 8) for dev in range(8)])  96.2 us
    reshape x1, local copies, waits for them, and re-layouts, local(): contrib.reshape(block_rows * block_slots, block_size, feature_width)  48.9 us
    reduce_scatter x1, waiting for transfers between devices, local(): lax.psum_scatter(panel_sum.astype(jnp.bfloat16), 'row', scatter_dimension...  47.4 us
    psum x1, blocking collectives, local(): weight_grad, bias_grad = lax.psum((weight_part, bias_part), ('row', 'col'))  44.5 us
    reduce_scatter x1, waiting for transfers between devices, local(): lax.psum_scatter(partial_value, 'col', scatter_dimension=0, tiled=True)  41.1 us
    dot_general x1, matrix products, local(): jnp.einsum('ikab,iaf->ikbf', tile_blocks, tile_grad.reshape(block_rows, b...  22.5 us
    all_gather x1, waiting for transfers between devices, local(): tile_grad = lax.all_gather(grad_agg, 'col', axis=0, tiled=True)  21 us
  transfers between devices with their start and end apart: 11, of which 10 were waited for; matrix products, arithmetic and copies ran while one was open for 38% of the time, Pallas kernels for 0%

profile of v1, /device:TPU:0, one launch (start us, length us, event | category | flops | bytes accessed | tf_op | source)
XLA Modules:
  0.0 505.9 jit_solution(11586907400195535935)
XLA Ops:
  7.2 3.0 collective-permute-start
  10.3 15.2 %collective-permute-done = bf16[1024,256]{1,0:T(8,128)(2,1)S(1)} collective-permute-done((bf16[1024,256]{1,0:T(8,128)(2,1)}, bf16[1024,256]{1,0:T(8,128)(2,1)S(1)}, u32[]{:S(2)}, u32[]{:S(2)}) %collective-permute-start) | collective-permute-done | bytes 524320 | tf_op jit(solution)/shard_map/ppermute | solution.py:18
  25.4 15.8 %collective-permute-done.1 = bf16[1024,256]{1,0:T(8,128)(2,1)S(1)} collective-permute-done((bf16[1024,256]{1,0:T(8,128)(2,1)S(1)}, bf16[1024,256]{1,0:T(8,128)(2,1)S(1)}, u32[]{:S(2)}, u32[]{:S(2)}) %collective-permute-start.1) | collective-permute-done | bytes 524320 | tf_op jit(solution)/shard_map/ppermute | solution.py:18
  41.2 14.9 %collective-permute-done.2 = bf16[1024,256]{1,0:T(8,128)(2,1)S(1)} collective-permute-done((bf16[1024,256]{1,0:T(8,128)(2,1)S(1)}, bf16[1024,256]{1,0:T(8,128)(2,1)S(1)}, u32[]{:S(2)}, u32[]{:S(2)}) %collective-permute-start.2) | collective-permute-done | bytes 524320 | tf_op jit(solution)/shard_map/ppermute | solution.py:18
  56.2 14.1 %collective-permute-done.3 = bf16[1024,256]{1,0:T(8,128)(2,1)S(1)} collective-permute-done((bf16[1024,256]{1,0:T(8,128)(2,1)S(1)}, bf16[1024,256]{1,0:T(8,128)(2,1)S(1)}, u32[]{:S(2)}, u32[]{:S(2)}) %collective-permute-start.3) | collective-permute-done | bytes 524320 | tf_op jit(solution)/shard_map/ppermute | solution.py:18
  70.2 13.2 %collective-permute-done.4 = bf16[1024,256]{1,0:T(8,128)(2,1)S(1)} collective-permute-done((bf16[1024,256]{1,0:T(8,128)(2,1)S(1)}, bf16[1024,256]{1,0:T(8,128)(2,1)S(1)}, u32[]{:S(2)}, u32[]{:S(2)}) %collective-permute-start.4) | collective-permute-done | bytes 524320 | tf_op jit(solution)/shard_map/ppermute | solution.py:18
  83.4 12.5 %collective-permute-done.5 = bf16[1024,256]{1,0:T(8,128)(2,1)} collective-permute-done((bf16[1024,256]{1,0:T(8,128)(2,1)S(1)}, bf16[1024,256]{1,0:T(8,128)(2,1)}, u32[]{:S(2)}, u32[]{:S(2)}) %collective-permute-start.5) | collective-permute-done | bytes 524320 | tf_op jit(solution)/shard_map/ppermute | solution.py:18
  97.6 10.5 %collective-permute-done.6 = bf16[1024,256]{1,0:T(8,128)(2,1)} collective-permute-done((bf16[1024,256]{1,0:T(8,128)(2,1)}, bf16[1024,256]{1,0:T(8,128)(2,1)}, u32[]{:S(2)}, u32[]{:S(2)}) %collective-permute-start.6) | collective-permute-done | bytes 524320 | tf_op jit(solution)/shard_map/ppermute | solution.py:18
  110.5 1.1 constant_dynamic-update-slice_fusion.8
  114.0 2.2 constant_dynamic-slice_fusion
  116.2 15.1 %gather_fusion = bf16[384,128,256]{2,1,0:T(8,128)(2,1)} fusion(bf16[64,128,256]{2,1,0:T(8,128)(2,1)} %bitcast.35, s32[1024]{0:T(1024)S(1)} %pad_clamp_fusion), kind=kCustom, calls=%fused_computation | custom fusion | bytes 50333184 | tf_op jit(solution)/shard_map/gather | solution.py:23
  131.4 16.1 %fusion = f32[32,256,128,1]{1,2,3,0:T(8,128)} fusion(bf16[32,12,128,256]{3,2,1,0:T(8,128)(2,1)} %bitcast.36, pred[32,12]{1,0:T(8,128)(4,1)S(1)} %iota_compare_fusion, bf16[32,1,12,128,128]{4,3,2,1,0:T(8,128)(2,1)} %param.8), kind=kOutput, calls=%fused_computation.2 | convolution fusion | flops 3233808384 | bytes 41943424 | tf_op jit(solution)/shard_map/ikab,ikbf->iaf/dot_general | solution.py:25
  147.6 41.1 %reduce-scatter.3.cloned.1.call-done = f32[1024,256]{1,0:T(8,128)} async-done(((f32[4096,256]{1,0:T(8,128)}), f32[1024,256]{1,0:T(8,128)}) %reduce-scatter.3.cloned.1.call-update) | async-done | bytes 1048592 | tf_op jit(solution)/shard_map/reduce_scatter | solution.py:29
  188.6 2.8 convert_reduce_fusion
  191.4 1.1 convolution_convert_fusion
  194.3 21.0 %all-gather.2.cloned.1.call-done = bf16[4096,256]{1,0:T(8,128)(2,1)} async-done(((bf16[1024,256]{1,0:T(8,128)(2,1)}), bf16[4096,256]{1,0:T(8,128)(2,1)}) %all-gather.2.cloned.1.call-update) | async-done | bytes 2097168 | tf_op jit(solution)/shard_map/all_gather | solution.py:43
  215.3 22.5 %fusion.3 = f32[32,256,12,128]{3,1,2,0:T(8,128)} fusion(bf16[32,128,256,1]{2,1,3,0:T(8,128)(2,1)} %bitcast.39, bf16[32,1,12,128,128]{4,3,2,1,0:T(8,128)(2,1)} %param.8), kind=kOutput, calls=%fused_computation.5 | convolution fusion | flops 3221225472 | bytes 65011712 | tf_op jit(solution)/shard_map/ikab,iaf->ikbf/dot_general | solution.py:44
  237.8 48.9 %copy.15 = f32[384,128,256]{2,1,0:T(8,128)} copy(f32[384,128,256]{1,2,0:T(8,128)} %bitcast.34) | data formatting | bytes 100663296 | tf_op jit(solution)/shard_map/reshape | solution.py:50
  286.7 4.3 broadcast_in_dim.23
  290.9 108.9 %scatter_fusion = f32[64,128,256]{2,1,0:T(8,128)} fusion(f32[64,128,256]{2,1,0:T(8,128)} %broadcast_in_dim.23, s32[384]{0:T(512)S(1)} %fusion.10, f32[384,128,256]{2,1,0:T(8,128)} %copy.15), kind=kCustom, calls=%fused_computation.1 | custom fusion | flops 12582912 | bytes 150996480 | tf_op jit(solution)/shard_map/scatter-add | solution.py:53
  399.8 5.9 %convert_element_type.29 = bf16[64,128,256]{2,1,0:T(8,128)(2,1)} convert(f32[64,128,256]{2,1,0:T(8,128)} %scatter_fusion) | non-fusion elementwise | flops 2097152 | bytes 12582912 | tf_op jit(solution)/shard_map/convert_element_type | solution.py:56
  405.8 44.5 %psum.15 = f32[256]{0:T(256)} all-reduce(f32[256]{0:T(256)S(1)} %get-tuple-element.4), channel_id=1, replica_groups=mesh['row'=8,'col'=4] {'row','col'}, use_global_device_ids=true, to_apply=%region_5.6 | all-reduce | flops 256 | bytes 2048 | tf_op jit(solution)/shard_map/psum | solution.py:42
  450.3 47.4 %reduce-scatter.5.cloned.1.call-done = bf16[1024,256]{1,0:T(8,128)(2,1)} async-done(((bf16[8192,256]{1,0:T(8,128)(2,1)}), bf16[1024,256]{1,0:T(8,128)(2,1)}) %reduce-scatter.5.cloned.1.call-update) | async-done | bytes 524304 | tf_op jit(solution)/shard_map/reduce_scatter | solution.py:55
  497.7 1.7 copy.37
  (54 shorter events, 8.2 us)
Async XLA Ops:
  7.2 181.5 %copy-start = (bf16[256,256]{1,0:T(8,128)(2,1)S(1)}, bf16[256,256]{1,0:T(8,128)(2,1)}, u32[]{:S(2)}) copy-start(bf16[256,256]{1,0:T(8,128)(2,1)} %param.11) | copy-start | bytes 393220
  7.2 106.8 %copy-start.2 = (bf16[1024,256]{1,0:T(8,128)(2,1)S(1)}, bf16[1024,256]{1,0:T(8,128)(2,1)}, u32[]{:S(2)}) copy-start(bf16[1024,256]{1,0:T(8,128)(2,1)} %param.7) | copy-start | bytes 1572868
  7.2 181.4 %reduce-scatter.3.cloned.1.call-start = ((), (), s32[]{:S(2)}) async-start(), calls=%async_computation.2 | async-start | bytes 5242880 | tf_op jit(solution)/shard_map/reduce_scatter | solution.py:29
  7.2 18.2 %collective-permute-start = (bf16[1024,256]{1,0:T(8,128)(2,1)}, bf16[1024,256]{1,0:T(8,128)(2,1)S(1)}, u32[]{:S(2)}, u32[]{:S(2)}) collective-permute-start(bf16[1024,256]{1,0:T(8,128)(2,1)} %param.7), channel_id=1, source_target_pairs={{0,4},{4,8},{8,12},{12,16},{16,20},{20,24},{24,28},{28,0},{1,5},{5... | collective-permute-start | bytes 1572872 | tf_op jit(solution)/shard_map/ppermute | solution.py:18
  25.4 15.8 %collective-permute-start.1 = (bf16[1024,256]{1,0:T(8,128)(2,1)S(1)}, bf16[1024,256]{1,0:T(8,128)(2,1)S(1)}, u32[]{:S(2)}, u32[]{:S(2)}) collective-permute-start(bf16[1024,256]{1,0:T(8,128)(2,1)S(1)} %collective-permute-done), channel_id=1, source_target_pairs={{0,4},{4,8},{8,12},{12,16},{16,20},{20,24},{24,28},{28,0},{1,5},{5... | collective-permute-start | bytes 1572872 | tf_op jit(solution)/shard_map/ppermute | solution.py:18
  41.2 14.9 %collective-permute-start.2 = (bf16[1024,256]{1,0:T(8,128)(2,1)S(1)}, bf16[1024,256]{1,0:T(8,128)(2,1)S(1)}, u32[]{:S(2)}, u32[]{:S(2)}) collective-permute-start(bf16[1024,256]{1,0:T(8,128)(2,1)S(1)} %collective-permute-done.1), channel_id=1, source_target_pairs={{0,4},{4,8},{8,12},{12,16},{16,20},{20,24},{24,28},{28,0},{1,5},{5... | collective-permute-start | bytes 1572872 | tf_op jit(solution)/shard_map/ppermute | solution.py:18
  56.1 14.1 %collective-permute-start.3 = (bf16[1024,256]{1,0:T(8,128)(2,1)S(1)}, bf16[1024,256]{1,0:T(8,128)(2,1)S(1)}, u32[]{:S(2)}, u32[]{:S(2)}) collective-permute-start(bf16[1024,256]{1,0:T(8,128)(2,1)S(1)} %collective-permute-done.2), channel_id=1, source_target_pairs={{0,4},{4,8},{8,12},{12,16},{16,20},{20,24},{24,28},{28,0},{1,5},{5... | collective-permute-start | bytes 1572872 | tf_op jit(solution)/shard_map/ppermute | solution.py:18
  70.2 13.2 %collective-permute-start.4 = (bf16[1024,256]{1,0:T(8,128)(2,1)S(1)}, bf16[1024,256]{1,0:T(8,128)(2,1)S(1)}, u32[]{:S(2)}, u32[]{:S(2)}) collective-permute-start(bf16[1024,256]{1,0:T(8,128)(2,1)S(1)} %collective-permute-done.3), channel_id=1, source_target_pairs={{0,4},{4,8},{8,12},{12,16},{16,20},{20,24},{24,28},{28,0},{1,5},{5... | collective-permute-start | bytes 1572872 | tf_op jit(solution)/shard_map/ppermute | solution.py:18
  83.4 12.5 %collective-permute-start.5 = (bf16[1024,256]{1,0:T(8,128)(2,1)S(1)}, bf16[1024,256]{1,0:T(8,128)(2,1)}, u32[]{:S(2)}, u32[]{:S(2)}) collective-permute-start(bf16[1024,256]{1,0:T(8,128)(2,1)S(1)} %collective-permute-done.4), channel_id=1, source_target_pairs={{0,4},{4,8},{8,12},{12,16},{16,20},{20,24},{24,28},{28,0},{1,5},{5... | collective-permute-start | bytes 1572872 | tf_op jit(solution)/shard_map/ppermute | solution.py:18
  95.9 12.2 %collective-permute-start.6 = (bf16[1024,256]{1,0:T(8,128)(2,1)}, bf16[1024,256]{1,0:T(8,128)(2,1)}, u32[]{:S(2)}, u32[]{:S(2)}) collective-permute-start(bf16[1024,256]{1,0:T(8,128)(2,1)} %collective-permute-done.5), channel_id=1, source_target_pairs={{0,4},{4,8},{8,12},{12,16},{16,20},{20,24},{24,28},{28,0},{1,5},{5... | collective-permute-start | bytes 1572872 | tf_op jit(solution)/shard_map/ppermute | solution.py:18
  131.4 57.3 %copy-start.5 = (bf16[1024,256]{1,0:T(8,128)(2,1)S(1)}, bf16[1024,256]{1,0:T(8,128)(2,1)}, u32[]{:S(2)}) copy-start(bf16[1024,256]{1,0:T(8,128)(2,1)} %param.13) | copy-start | bytes 1572868
  131.4 57.3 %copy-start.6 = (f32[256]{0:T(256)S(1)}, f32[256]{0:T(256)}, u32[]{:S(2)}) copy-start(f32[256]{0:T(256)} %param.12) | copy-start | bytes 3076
  147.5 45.3 %copy-start.4 = (s32[32,1,12]{0,1,2:T(1,128)S(1)}, s32[32,1,12]{0,1,2:T(1,128)}, u32[]{:S(2)}) copy-start(s32[32,1,12]{0,1,2:T(1,128)} %param.9) | copy-start | bytes 4612
  147.5 67.8 %all-gather.2.cloned.1.call-start = ((), (), s32[]{:S(2)}) async-start(), calls=%async_computation.3 | async-start | bytes 2621440 | tf_op jit(solution)/shard_map/all_gather | solution.py:43
  188.6 4.3 copy-start.3
  192.6 257.7 %all-reduce.2.cloned.1.call-start = ((), (), s32[]{:S(2)}) async-start(), calls=%async_computation.5 | async-start | bytes 524288 | tf_op jit(solution)/shard_map/psum | solution.py:42
  194.0 303.7 %reduce-scatter.5.cloned.1.call-start = ((), (), s32[]{:S(2)}) async-start(), calls=%async_computation.4 | async-start | bytes 4718592 | tf_op jit(solution)/shard_map/reduce_scatter | solution.py:55
  290.9 208.5 %copy-start.1 = (bf16[256,256]{1,0:T(8,128)(2,1)S(1)}, bf16[256,256]{1,0:T(8,128)(2,1)}, u32[]{:S(2)}) copy-start(bf16[256,256]{1,0:T(8,128)(2,1)} %param.11) | copy-start | bytes 393220
Sparse Core Ops, SparseCore 0:
  147.6 40.9 reduce-scatter.2
  192.7 22.5 all-gather.1
  221.4 126.5 all-reduce.1
  405.9 91.7 reduce-scatter.4
